TPU v7x, 32 devices: a whole 2x2x4 slice. The times are simulated.
32 devices in a mesh: uly: 2 (over x), blk: 8 (over z, y), dp: 2 (over core).
Axes of the slice: x: 2, y: 2, z: 4, core: 2. Of those that a mesh axis runs over, the one named last changes fastest.
Arguments:
- queries: bfloat16 [2, 2048, 1024], P('dp', ('blk', 'uly')), may hold values from -6 to 6
- out_grad: bfloat16 [2, 2048, 1024], P('dp', ('blk', 'uly')), may hold values from -6 to 6
- keys_values: bfloat16 [2, 2048, 256], P('dp', ('blk', 'uly')), may hold values from -9 to 9
- attn_output: bfloat16 [2, 8, 2048, 128], P('dp', 'uly', 'blk'), may hold values from -6 to 6
- logsumexp: float32 [2, 8, 2048], P('dp', 'uly', 'blk'), may hold values from 7 to 9
- segments: int32 [2, 2048], P('dp'), may hold values from 0 to 15, never falling along the last dimension, each value on 1 to 256 neighbouring positions
- layer_input: bfloat16 [2, 2048, 4096], P('dp', ('blk', 'uly')), may hold values from -6 to 6
Outputs:
- query_grad: bfloat16 [2, 2048, 1024], P('dp', ('blk', 'uly'))
- keyvalue_grad: bfloat16 [2, 2048, 256], P('dp', ('blk', 'uly'))
- weight_grad: float32 [4096, 128], P(('uly', 'blk', 'dp'))
Inputs may be any that keep to these rules, and one draw needn't show every extreme that they name: `segments`: document ids never fall along a sequence; each id covers 1 to 256 positions, and some id covers exactly that many.
All inputs are finite; a program needn't handle non-finite values.
Results may differ from a plain program's by a relative error of at most 0.0059.
Values may be sent and summed in bfloat16 or wider, within the bound.
A program may use at most 64 MiB of HBM per device.

v0:
```python
import jax
import jax.numpy as jnp
from jax import lax
from jax.sharding import PartitionSpec as P


def passed_along(shard, axis, by):
    devices = lax.axis_size(axis)
    pairs = [(i, i + by) for i in range(devices) if 0 <= i + by < devices]
    return lax.ppermute(shard, axis, pairs)


def block_grads(
    query_rows, grad_rows, lse_rows, delta_rows, query_start, key_block, key_start, seq_ids, live
):
    block_rows = query_rows.shape[0]
    local_heads = lse_rows.shape[0]
    head_dim = key_block.shape[1] // 2
    key_rows = key_block.shape[0]
    seq_len = seq_ids.shape[0]
    tile_rows = min(512, block_rows)
    tile_count = block_rows // tile_rows
    scale = head_dim ** (-0.5)
    query_tiles = query_rows.reshape(tile_count, tile_rows, local_heads, head_dim)
    grad_tiles = grad_rows.reshape(tile_count, tile_rows, local_heads, head_dim)
    lse_tiles = lse_rows.reshape(local_heads, tile_count, tile_rows).transpose(1, 0, 2)
    delta_tiles = delta_rows.reshape(local_heads, tile_count, tile_rows).transpose(1, 0, 2)
    keys_part = key_block[:, :head_dim]
    values_part = key_block[:, head_dim:]
    key_pos = key_start + jnp.arange(key_rows, dtype=jnp.int32)
    key_seg = lax.dynamic_slice_in_dim(
        seq_ids, jnp.clip(key_start, 0, seq_len - key_rows), key_rows, 0
    )

    def tile_step(carry, pieces):
        tile_index, query_tile, grad_tile, lse_tile, delta_tile = pieces
        tile_start = query_start + tile_index * tile_rows
        query_pos = tile_start + jnp.arange(tile_rows, dtype=jnp.int32)
        query_seg = lax.dynamic_slice_in_dim(
            seq_ids, jnp.clip(tile_start, 0, seq_len - tile_rows), tile_rows, 0
        )
        visible = (
            live
            & (key_seg[None, :] == query_seg[:, None])
            & (key_pos[None, :] <= query_pos[:, None])
        )
        scores = (
            jnp.einsum("qhd,kd->hqk", query_tile, keys_part, preferred_element_type=jnp.float32)
            * scale
        )
        probs = jnp.where(visible[None], jnp.exp(scores - lse_tile[:, :, None]), 0.0)
        dprobs = jnp.einsum(
            "qhd,kd->hqk", grad_tile, values_part, preferred_element_type=jnp.float32
        )
        dscores = probs * (dprobs - delta_tile[:, :, None])
        probs_low = probs.astype(jnp.bfloat16)
        dscores_low = dscores.astype(jnp.bfloat16)
        query_part = (
            jnp.einsum("hqk,kd->qhd", dscores_low, keys_part, preferred_element_type=jnp.float32)
            * scale
        )
        key_part = (
            jnp.einsum("hqk,qhd->kd", dscores_low, query_tile, preferred_element_type=jnp.float32)
            * scale
        )
        value_part = jnp.einsum(
            "hqk,qhd->kd", probs_low, grad_tile, preferred_element_type=jnp.float32
        )
        query_part, kv_part = (query_part, jnp.concatenate([key_part, value_part], axis=1))
        return (carry + kv_part, query_part)

    start_total = jnp.zeros((key_rows, 2 * head_dim), jnp.float32)
    kv_total, query_parts = lax.scan(
        tile_step,
        start_total,
        (jnp.arange(tile_count, dtype=jnp.int32), query_tiles, grad_tiles, lse_tiles, delta_tiles),
    )
    return (query_parts.reshape(block_rows, local_heads * head_dim), kv_total)


def on_device(queries, out_grad, keys_values, attn_output, logsumexp, segments, layer_input):
    head_dim = keys_values.shape[2] // 2
    query_heads, grad_heads = (
        lax.all_to_all(queries, "uly", split_axis=2, concat_axis=1, tiled=True),
        lax.all_to_all(out_grad, "uly", split_axis=2, concat_axis=1, tiled=True),
    )
    key_block = lax.all_gather(keys_values, "uly", axis=1, tiled=True)[0]
    query_rows = query_heads[0]
    grad_rows = grad_heads[0]
    block_rows = query_rows.shape[0]
    local_heads = attn_output.shape[1]
    lse_rows = logsumexp[0]
    delta_rows = jnp.einsum(
        "thd,htd->ht",
        grad_rows.reshape(block_rows, local_heads, head_dim),
        attn_output[0],
        preferred_element_type=jnp.float32,
    )
    seq_ids = segments[0]
    cycle_index = lax.axis_index("blk")
    own_start = cycle_index * block_rows
    always_live = jnp.asarray(True)
    query_own, kv_own = block_grads(
        query_rows,
        grad_rows,
        lse_rows,
        delta_rows,
        own_start,
        key_block,
        own_start,
        seq_ids,
        always_live,
    )
    key_before = passed_along(key_block, "blk", 1)
    query_before, kv_before = block_grads(
        query_rows,
        grad_rows,
        lse_rows,
        delta_rows,
        own_start,
        key_before,
        own_start - block_rows,
        seq_ids,
        cycle_index >= 1,
    )
    kv_returned = passed_along(kv_before, "blk", -1)
    query_total = query_own + query_before
    kv_total = kv_own + kv_returned
    kv_sums = lax.psum_scatter(kv_total, "uly", scatter_dimension=0, tiled=True)
    kv_grad = kv_sums.astype(jnp.bfloat16)
    query_grad = lax.all_to_all(
        query_total.astype(jnp.bfloat16)[None], "uly", split_axis=1, concat_axis=2, tiled=True
    )
    value_grads = kv_grad[:, head_dim:]
    all_devices = lax.axis_size(("uly", "blk", "dp"))
    total_tokens = layer_input.shape[1] * all_devices
    flat_input = layer_input[0]
    weight_sum = lax.psum_scatter(
        lax.dot_general(
            flat_input, value_grads, (((0,), (0,)), ((), ())), preferred_element_type=jnp.float32
        ),
        ("uly", "blk", "dp"),
        scatter_dimension=0,
        tiled=True,
    )
    return (query_grad, kv_grad[None], weight_sum * total_tokens ** (-0.5))


def solution(mesh):
    placed = (
        P("dp", ("blk", "uly"), None),
        P("dp", ("blk", "uly"), None),
        P("dp", ("blk", "uly"), None),
        P("dp", "uly", "blk", None),
        P("dp", "uly", "blk"),
        P("dp", None),
        P("dp", ("blk", "uly"), None),
    )
    return jax.shard_map(
        on_device,
        mesh=mesh,
        in_specs=placed,
        out_specs=(
            P("dp", ("blk", "uly"), None),
            P("dp", ("blk", "uly"), None),
            P(("uly", "blk", "dp"), None),
        ),
        check_vma=False,
    )
```

profile of v0, /device:TPU:0, one launch (start us, length us, event | category | flops | bytes accessed | tf_op | source)
XLA Modules:
  0.0 211.1 jit_solution(4560425027189386302)
XLA Ops:
  7.2 6.2 %all_gather.3 = bf16[1,256,256]{2,1,0:T(8,128)(2,1)S(1)} all-gather(bf16[1,128,256]{2,1,0:T(8,128)(2,1)} %param.9), channel_id=1, replica_groups=mesh['uly'=2,'blk'=8,'dp'=2] {'uly'}, dimensions={1}, use_global_device_ids=true | all-gather | bytes 196608 | tf_op jit(solution)/shard_map/all_gather | solution.py:87
  13.4 3.9 %collective-permute-start = (bf16[256,256]{1,0:T(8,128)(2,1)S(1)}, bf16[256,256]{1,0:T(8,128)(2,1)S(1)}, u32[]{:S(2)}, u32[]{:S(2)}) collective-permute-start(bf16[256,256]{1,0:T(8,128)(2,1)S(1)} %bitcast.121), channel_id=1, source_target_pairs={{0,2},{2,4},{4,6},{6,8},{8,10},{10,12},{12,14},{1,3},{3,5},{5,7},{... | collective-permute-start | bytes 393224 | tf_op jit(solution)/shard_map/ppermute | solution.py:10
  17.4 1.3 copy.96
  19.1 2.2 %reduce.3 = bf16[1024,128]{1,0:T(8,128)(2,1)S(1)} reduce(bf16[1024,1,128]{2,1,0:T(2,128)(2,1)S(1)} %bitcast.113, bf16[]{:T(256)} %broadcast.125), dimensions={1}, to_apply=%bitcast.93.reduce_sub_computation | reduce | bytes 524290
  21.4 0.8 reshape.193
  22.1 3.4 %all-to-all-start.1 = ((bf16[2,2,32768]{2,1,0:T(2,128)(2,1)}), bf16[2,2,32768]{2,1,0:T(2,128)(2,1)S(1)}, u32[]{:S(2)}, u32[]{:S(2)}) async-start(bf16[2,2,32768]{2,1,0:T(2,128)(2,1)} %reshape.193), calls=%async_computation.1 | async-start | bytes 524288 | tf_op jit(solution)/shard_map/all_to_all | solution.py:85
  26.0 2.2 %reduce.2 = bf16[1024,128]{1,0:T(8,128)(2,1)S(1)} reduce(bf16[1024,1,128]{2,1,0:T(2,128)(2,1)S(1)} %bitcast.115, bf16[]{:T(256)} %broadcast.125), dimensions={1}, to_apply=%bitcast.91.reduce_sub_computation | reduce | bytes 524290
  28.2 0.8 reshape.191
  29.0 0.8 constant_dynamic-slice_fusion
  30.7 3.4 %all-to-all-start = ((bf16[2,2,32768]{2,1,0:T(2,128)(2,1)}), bf16[2,2,32768]{2,1,0:T(2,128)(2,1)S(1)}, u32[]{:S(2)}, u32[]{:S(2)}) async-start(bf16[2,2,32768]{2,1,0:T(2,128)(2,1)} %reshape.191), calls=%async_computation | async-start | bytes 524288 | tf_op jit(solution)/shard_map/all_to_all | solution.py:84
  35.0 4.3 %all-to-all-done = bf16[2,2,32768]{2,1,0:T(2,128)(2,1)S(1)} async-done(((bf16[2,2,32768]{2,1,0:T(2,128)(2,1)}), bf16[2,2,32768]{2,1,0:T(2,128)(2,1)S(1)}, u32[]{:S(2)}, u32[]{:S(2)}) %all-to-all-start) | async-done | bytes 262176 | tf_op jit(solution)/shard_map/all_to_all | solution.py:84
  41.7 1.3 collective-permute-start.1
  44.3 5.7 %collective-permute-done.1 = f32[256,256]{0,1:T(8,128)S(1)} collective-permute-done((f32[256,256]{0,1:T(8,128)S(1)}, f32[256,256]{0,1:T(8,128)S(1)}, u32[]{:S(2)}, u32[]{:S(2)}) %collective-permute-start.1) | collective-permute-done | bytes 262176 | tf_op jit(solution)/shard_map/ppermute | solution.py:10
  49.9 0.7 maximum_add_fusion
  50.7 12.0 %reduce-scatter.3.cloned.1.call-done = f32[128,256]{0,1:T(8,128)} async-done(((f32[256,256]{0,1:T(8,128)}), f32[128,256]{0,1:T(8,128)}) %reduce-scatter.3.cloned.1.call-update) | async-done | bytes 131088 | tf_op jit(solution)/shard_map/reduce_scatter | solution.py:129
  62.7 0.9 convert_element_type.42
  63.6 1.8 convolution_bitcast_fusion
  66.5 2.2 %reduce.4 = bf16[256,512]{1,0:T(8,128)(2,1)S(1)} reduce(bf16[256,1,512]{2,1,0:T(2,128)(2,1)S(1)} %bitcast.114, bf16[]{:T(256)} %broadcast.125), dimensions={1}, to_apply=%bitcast.95.reduce_sub_computation | reduce | bytes 524290
  68.9 7.8 %all_to_all.48 = bf16[2,2,32768]{2,1,0:T(2,128)(2,1)S(1)} all-to-all(bf16[2,2,32768]{2,1,0:T(2,128)(2,1)S(1)} %reshape.195), channel_id=1, replica_groups=mesh['uly'=2,'blk'=8,'dp'=2] {'uly'}, dimensions={0} | all-to-all | bytes 524288 | tf_op jit(solution)/shard_map/all_to_all | solution.py:131
  77.2 0.9 copy.115
  78.1 0.7 copy.116
  78.9 123.8 %reduce-scatter.5.cloned.1.call-done = f32[128,128]{0,1:T(8,128)} async-done(((f32[4096,128]{0,1:T(8,128)}), f32[128,128]{0,1:T(8,128)}) %reduce-scatter.5.cloned.1.call-update) | async-done | bytes 65552 | tf_op jit(solution)/shard_map/reduce_scatter | solution.py:138
  202.6 0.8 broadcast_multiply_fusion
  203.5 0.7 copy.117
  (48 shorter events, 7.9 us)
Async XLA Ops:
  7.2 56.5 %copy-start = (bf16[1,128,4096]{2,1,0:T(8,128)(2,1)S(1)}, bf16[1,128,4096]{2,1,0:T(8,128)(2,1)}, u32[]{:S(2)}) copy-start(bf16[1,128,4096]{2,1,0:T(8,128)(2,1)} %param.13) | copy-start | bytes 3145732
  7.2 18.4 %copy-start.2 = (bf16[1,128,1024]{2,1,0:T(8,128)(2,1)S(1)}, bf16[1,128,1024]{2,1,0:T(8,128)(2,1)}, u32[]{:S(2)}) copy-start(bf16[1,128,1024]{2,1,0:T(8,128)(2,1)} %param.7) | copy-start | bytes 786436
  13.4 26.9 %collective-permute-start = (bf16[256,256]{1,0:T(8,128)(2,1)S(1)}, bf16[256,256]{1,0:T(8,128)(2,1)S(1)}, u32[]{:S(2)}, u32[]{:S(2)}) collective-permute-start(bf16[256,256]{1,0:T(8,128)(2,1)S(1)} %bitcast.121), channel_id=1, source_target_pairs={{0,2},{2,4},{4,6},{6,8},{8,10},{10,12},{12,14},{1,3},{3,5},{5,7},{... | collective-permute-start | bytes 393224 | tf_op jit(solution)/shard_map/ppermute | solution.py:10
  22.1 8.6 %all-to-all-start.1 = ((bf16[2,2,32768]{2,1,0:T(2,128)(2,1)}), bf16[2,2,32768]{2,1,0:T(2,128)(2,1)S(1)}, u32[]{:S(2)}, u32[]{:S(2)}) async-start(bf16[2,2,32768]{2,1,0:T(2,128)(2,1)} %reshape.193), calls=%async_computation.1 | async-start | bytes 524288 | tf_op jit(solution)/shard_map/all_to_all | solution.py:85
  30.7 8.6 %all-to-all-start = ((bf16[2,2,32768]{2,1,0:T(2,128)(2,1)}), bf16[2,2,32768]{2,1,0:T(2,128)(2,1)S(1)}, u32[]{:S(2)}, u32[]{:S(2)}) async-start(bf16[2,2,32768]{2,1,0:T(2,128)(2,1)} %reshape.191), calls=%async_computation | async-start | bytes 524288 | tf_op jit(solution)/shard_map/all_to_all | solution.py:84
  34.2 28.6 %reduce-scatter.3.cloned.1.call-start = ((), (), s32[]{:S(2)}) async-start(), calls=%async_computation.5 | async-start | bytes 393216 | tf_op jit(solution)/shard_map/reduce_scatter | solution.py:129
  34.8 5.3 %copy-start.3 = (bf16[1,4,256,128]{3,2,1,0:T(8,128)(2,1)S(1)}, bf16[1,4,256,128]{3,2,1,0:T(8,128)(2,1)}, u32[]{:S(2)}) copy-start(bf16[1,4,256,128]{3,2,1,0:T(8,128)(2,1)} %param.10) | copy-start | bytes 786436
  35.0 5.4 %copy-start.4 = (f32[1,4,256]{2,1,0:T(4,128)S(1)}, f32[1,4,256]{2,1,0:T(4,128)}, u32[]{:S(2)}) copy-start(f32[1,4,256]{2,1,0:T(4,128)} %param.11) | copy-start | bytes 12292
  41.7 8.3 %collective-permute-start.1 = (f32[256,256]{0,1:T(8,128)S(1)}, f32[256,256]{0,1:T(8,128)S(1)}, u32[]{:S(2)}, u32[]{:S(2)}) collective-permute-start(f32[256,256]{0,1:T(8,128)S(1)} %pad_maximum_fusion), channel_id=1, source_target_pairs={{2,0},{4,2},{6,4},{8,6},{10,8},{12,10},{14,12},{3,1},{5,3},{7,5},{... | collective-permute-start | bytes 786440 | tf_op jit(solution)/shard_map/ppermute | solution.py:10
  50.7 152.0 %reduce-scatter.5.cloned.1.call-start = ((), (), s32[]{:S(2)}) async-start(), calls=%async_computation.6 | async-start | bytes 2162688 | tf_op jit(solution)/shard_map/reduce_scatter | solution.py:138
  66.5 11.6 %copy-start.1 = (f32[128,256]{0,1:T(8,128)S(1)}, f32[128,256]{0,1:T(8,128)}, u32[]{:S(2)}) copy-start(f32[128,256]{0,1:T(8,128)} %reduce-scatter.3.cloned.1.call-done) | copy-start | bytes 393220
Sparse Core Ops, SparseCore 0:
  50.8 11.8 reduce-scatter.2
  65.6 137.0 reduce-scatter.4
where the time goes:
time: 212 us; the launch traced here: 211 us
  waiting for transfers between devices  146 us (69%)
  between operations  14.4 us (7%)
  blocking collectives  14.1 us (7%)
  starting transfers between devices  12.2 us (6%)
  other arithmetic  9.67 us (5%)
  local copies, waits for them, and re-layouts  9.44 us (4%)
  matrix products  4.83 us (2%)
    reduce_scatter x1, waiting for transfers between devices, on_device(): lax.psum_scatter(lax.dot_general(flat_input, value_grads, (((0,), (0,)),...  124 us
    reduce_scatter x1, waiting for transfers between devices, on_device(): kv_sums = lax.psum_scatter(kv_total, 'uly', scatter_dimension=0, tiled=True)  12 us
    all_to_all x1, blocking collectives, on_device(): lax.all_to_all(query_total.astype(jnp.bfloat16)[None], 'uly', split_axis=...  7.84 us
    unnamed x25, local copies, waits for them, and re-layouts  7.15 us
    unnamed x4, other arithmetic  6.72 us
    all_gather x1, blocking collectives, on_device(): key_block = lax.all_gather(keys_values, 'uly', axis=1, tiled=True)[0]  6.24 us
    ppermute x2, waiting for transfers between devices, passed_along(): return lax.ppermute(shard, axis, pairs)  5.67 us
    ppermute x2, starting transfers between devices, passed_along(): return lax.ppermute(shard, axis, pairs)  5.2 us
  transfers between devices with their start and end apart: 6, of which 5 were waited for; matrix products, arithmetic and copies ran while one was open for 8% of the time, Pallas kernels for 0%

commit v1 on v0

--- a/solution.py
+++ b/solution.py
@@ -1,7 +1,312 @@
 import jax
 import jax.numpy as jnp
 from jax import lax
+from jax.experimental import pallas as pl
+from jax.experimental.pallas import tpu as pltpu
 from jax.sharding import PartitionSpec as P
+
+MESH = pl.DeviceIdType.MESH
+HEAD = 128
+HEADS = 8
+CHUNK = 128
+CHUNKS = 16
+SLOTS = 3
+GROUP = 16
+HIDDEN = -1e30
+
+
+def fused_kernel(
+    q_hbm,
+    g_hbm,
+    kv_hbm,
+    o_hbm,
+    lse_hbm,
+    seg_ref,
+    x_hbm,
+    dq_ref,
+    dkv_ref,
+    w_ref,
+    qs,
+    gs,
+    kvb,
+    ob,
+    lb,
+    p_all,
+    ds_all,
+    send_kv,
+    recv_kv,
+    xin,
+    vg,
+    part,
+    part_in,
+    q_sem,
+    g_sem,
+    own_sem,
+    x_own_sem,
+    kv_send,
+    kv_recv,
+    o_send,
+    o_recv,
+    ret_send,
+    ret_recv,
+    x_send,
+    x_recv,
+    v_send,
+    v_recv,
+    p_send,
+    p_recv,
+):
+    rows, head_dim = CHUNK, HEAD
+    uly = lax.axis_index("uly")
+    blk = lax.axis_index("blk")
+    dp = lax.axis_index("dp")
+    chunk = blk * 2 + uly
+    half = blk // 4
+    member = uly * 8 + (blk % 4) * 2 + dp
+
+    def at_chunk(index):
+        index = lax.rem(index + CHUNKS, CHUNKS)
+        return {"uly": index % 2, "blk": index // 2, "dp": dp}
+
+    def at_member(index):
+        index = lax.rem(index, GROUP)
+        return {"uly": index // 8, "blk": half * 4 + (index % 8) // 2, "dp": index % 2}
+
+    across = {"uly": 1 - uly, "blk": blk, "dp": dp}
+    mirror = {"uly": uly, "blk": lax.rem(blk + 4, 8), "dp": dp}
+
+    def cols_of(index, side):
+        index = lax.rem(index, GROUP)
+        return pl.ds(pl.multiple_of(((index // 8) * 16 + side * 8 + index % 8) * 128, 128), 128)
+
+    loads = []
+    for h in range(HEADS):
+        at_rows, at_cols = pl.ds(h * rows, rows), pl.ds(h * head_dim, head_dim)
+        loads.append(pltpu.make_async_copy(q_hbm.at[:, at_cols], qs.at[at_rows], q_sem.at[h]))
+        loads.append(pltpu.make_async_copy(g_hbm.at[:, at_cols], gs.at[at_rows], g_sem.at[h]))
+    mine = pl.ds(pl.multiple_of(uly * rows, rows), rows)
+    theirs = pl.ds(pl.multiple_of((1 - uly) * rows, rows), rows)
+    loads.append(pltpu.make_async_copy(kv_hbm, kvb.at[pl.ds(0, rows)], own_sem.at[0]))
+    loads.append(pltpu.make_async_copy(o_hbm.at[:, mine], ob.at[uly], own_sem.at[1]))
+    loads.append(pltpu.make_async_copy(lse_hbm.at[:, mine], lb.at[uly], own_sem.at[2]))
+    for copy in loads:
+        copy.start()
+    x_own = [
+        pltpu.make_async_copy(x_hbm.at[:, cols_of(member, side)], xin.at[side, 0], x_own_sem.at[side])
+        for side in range(2)
+    ]
+    for copy in x_own:
+        copy.start()
+
+    barrier = pltpu.get_barrier_semaphore()
+    for step in (1, 2, -1, -2):
+        pl.semaphore_signal(barrier, inc=1, device_id=at_chunk(chunk + step), device_id_type=MESH)
+    pl.semaphore_signal(barrier, inc=1, device_id=mirror, device_id_type=MESH)
+    for k in range(1, GROUP):
+        pl.semaphore_signal(barrier, inc=1, device_id=at_member(member + k), device_id_type=MESH)
+    pl.semaphore_wait(barrier, GROUP - 1 + 5)
+
+    def remote(src, dst, send, recv, device):
+        return pltpu.make_async_remote_copy(
+            src_ref=src,
+            dst_ref=dst,
+            send_sem=send,
+            recv_sem=recv,
+            device_id=device,
+            device_id_type=MESH,
+        )
+
+    kv_out = [
+        remote(
+            kv_hbm, kvb.at[pl.ds(s * rows, rows)], kv_send.at[s - 1], kv_recv.at[s - 1], at_chunk(chunk + s)
+        )
+        for s in (1, 2)
+    ]
+    o_out = [
+        remote(o_hbm.at[:, theirs], ob.at[uly], o_send.at[0], o_recv.at[0], across),
+        remote(lse_hbm.at[:, theirs], lb.at[uly], o_send.at[1], o_recv.at[1], across),
+    ]
+    for copy in kv_out + o_out:
+        copy.start()
+    x_out = [
+        remote(
+            x_hbm.at[:, cols_of(member + k, side)],
+            xin.at[side, k],
+            x_send.at[side, k],
+            x_recv.at[side, k],
+            at_member(member + k),
+        )
+        for k in range(1, GROUP)
+        for side in range(2)
+    ]
+    for copy in x_out:
+        copy.start()
+
+    lane_query = lax.broadcasted_iota(jnp.int32, (rows, rows), 1)
+    row_key = lax.broadcasted_iota(jnp.int32, (rows, rows), 0)
+
+    def seg_row(index):
+        index = lax.rem(index + CHUNKS, CHUNKS)
+        return seg_ref[:, pl.ds(pl.multiple_of(index * rows, rows), rows)]
+
+    own_seg = jnp.broadcast_to(seg_row(chunk), (rows, rows))
+    biases = []
+    for s in range(SLOTS):
+        key_seg = jnp.broadcast_to(seg_row(chunk - s), (rows, rows)).T
+        seen = (key_seg == own_seg) & (chunk >= s)
+        if s == 0:
+            seen = seen & (row_key <= lane_query)
+        biases.append(jnp.where(seen, 0.0, HIDDEN))
+    bias = jnp.concatenate(biases, axis=0)
+    bias = jnp.concatenate([bias, bias], axis=1)
+
+    for copy in loads:
+        copy.wait()
+    for copy in o_out + kv_out:
+        copy.wait_recv()
+    scale = head_dim ** (-0.5)
+    across_dims = (((1,), (1,)), ((), ()))
+    keys = kvb[:, :head_dim]
+    values = kvb[:, head_dim:]
+    for pair in range(HEADS // 2):
+        at_rows = slice(pair * 2 * rows, (pair + 1) * 2 * rows)
+        q_pair = qs[at_rows, :]
+        g_pair = gs[at_rows, :]
+        deltas, lses = [], []
+        for h in (2 * pair, 2 * pair + 1):
+            prods = lax.dot_general(
+                ob[h // 4, h % 4],
+                gs[h * rows : (h + 1) * rows, :],
+                across_dims,
+                preferred_element_type=jnp.float32,
+            )
+            deltas.append(
+                jnp.sum(jnp.where(row_key == lane_query, prods, 0.0), axis=0, keepdims=True)
+            )
+            lses.append(lb[h // 4, h % 4 : h % 4 + 1, :])
+        delta = jnp.concatenate(deltas, axis=1)
+        lse = jnp.concatenate(lses, axis=1)
+        scores = lax.dot_general(keys, q_pair, across_dims, preferred_element_type=jnp.float32)
+        dprob = lax.dot_general(values, g_pair, across_dims, preferred_element_type=jnp.float32)
+        prob = jnp.exp(scores * scale - lse + bias)
+        p_all[:, at_rows] = prob.astype(jnp.bfloat16)
+        ds_all[:, at_rows] = (prob * (dprob - delta)).astype(jnp.bfloat16)
+
+    dk = jnp.dot(ds_all[rows:, :], qs[...], preferred_element_type=jnp.float32) * scale
+    send_kv[:, :, :head_dim] = dk.reshape(2, rows, head_dim)
+    dv = jnp.dot(p_all[rows:, :], gs[...], preferred_element_type=jnp.float32)
+    send_kv[:, :, head_dim:] = dv.reshape(2, rows, head_dim)
+    returns = [
+        remote(send_kv.at[s - 1], recv_kv.at[s - 1], ret_send.at[s - 1], ret_recv.at[s - 1], at_chunk(chunk - s))
+        for s in (1, 2)
+    ]
+    for copy in returns:
+        copy.start()
+    dv_own = jnp.dot(p_all[:rows, :], gs[...], preferred_element_type=jnp.float32)
+    dk_own = jnp.dot(ds_all[:rows, :], qs[...], preferred_element_type=jnp.float32) * scale
+    for h in range(HEADS):
+        at_rows = slice(h * rows, (h + 1) * rows)
+        dq = lax.dot_general(
+            ds_all[:, at_rows], keys, (((0,), (0,)), ((), ())), preferred_element_type=jnp.float32
+        )
+        dq_ref[:, at_rows] = (dq * scale).astype(jnp.bfloat16)
+
+    for copy in returns:
+        copy.wait_recv()
+    value_grad = (dv_own + recv_kv[0, :, head_dim:] + recv_kv[1, :, head_dim:]).astype(jnp.bfloat16)
+    vg[0] = value_grad
+    v_out = [
+        remote(vg.at[0], vg.at[k], v_send.at[k], v_recv.at[k], at_member(member + k))
+        for k in range(1, GROUP)
+    ]
+    for copy in v_out:
+        copy.start()
+    dkv_ref[:, head_dim:] = value_grad
+    dkv_ref[:, :head_dim] = (dk_own + recv_kv[0, :, :head_dim] + recv_kv[1, :, :head_dim]).astype(
+        jnp.bfloat16
+    )
+
+    for copy in x_own:
+        copy.wait()
+    for copy in x_out:
+        copy.wait_recv()
+    for copy in v_out:
+        copy.wait_recv()
+    grads = vg[...].reshape(GROUP * rows, head_dim)
+    for side in range(2):
+        part[side] = lax.dot_general(
+            xin[side].reshape(GROUP * rows, 128),
+            grads,
+            (((0,), (0,)), ((), ())),
+            preferred_element_type=jnp.float32,
+        )
+    swap = remote(part.at[1 - half], part_in, p_send.at[0], p_recv.at[0], mirror)
+    swap.start()
+    swap.wait_recv()
+    w_ref[...] = (part[half] + part_in[...]) * (rows * CHUNKS * 2) ** (-0.5)
+    for copy in kv_out + o_out + x_out + returns + v_out + [swap]:
+        copy.wait_send()
+
+
+def fused(queries, out_grad, keys_values, attn_output, logsumexp, segments, layer_input):
+    anywhere = pl.BlockSpec(memory_space=pl.ANY)
+    in_vmem = pl.BlockSpec(memory_space=pltpu.VMEM)
+    low, full = jnp.bfloat16, jnp.float32
+    dma = pltpu.SemaphoreType.DMA
+    width = HEADS * HEAD
+    dq, dkv, weight = pl.pallas_call(
+        fused_kernel,
+        out_shape=(
+            jax.ShapeDtypeStruct((CHUNK, width), low),
+            jax.ShapeDtypeStruct((CHUNK, 2 * HEAD), low),
+            jax.ShapeDtypeStruct((128, HEAD), full),
+        ),
+        in_specs=[anywhere] * 5 + [in_vmem, anywhere],
+        out_specs=(in_vmem, in_vmem, in_vmem),
+        scratch_shapes=[
+            pltpu.VMEM((width, HEAD), low),
+            pltpu.VMEM((width, HEAD), low),
+            pltpu.VMEM((SLOTS * CHUNK, 2 * HEAD), low),
+            pltpu.VMEM((2, HEADS // 2, CHUNK, HEAD), low),
+            pltpu.VMEM((2, HEADS // 2, CHUNK), full),
+            pltpu.VMEM((SLOTS * CHUNK, width), low),
+            pltpu.VMEM((SLOTS * CHUNK, width), low),
+            pltpu.VMEM((2, CHUNK, 2 * HEAD), full),
+            pltpu.VMEM((2, CHUNK, 2 * HEAD), full),
+            pltpu.VMEM((2, GROUP, CHUNK, 128), low),
+            pltpu.VMEM((GROUP, CHUNK, HEAD), low),
+            pltpu.VMEM((2, 128, HEAD), full),
+            pltpu.VMEM((128, HEAD), full),
+            dma((HEADS,)),
+            dma((HEADS,)),
+            dma((3,)),
+            dma((2,)),
+            dma((2,)),
+            dma((2,)),
+            dma((2,)),
+            dma((2,)),
+            dma((2,)),
+            dma((2,)),
+            dma((2, GROUP)),
+            dma((2, GROUP)),
+            dma((GROUP,)),
+            dma((GROUP,)),
+            dma((1,)),
+            dma((1,)),
+        ],
+        compiler_params=pltpu.CompilerParams(
+            collective_id=0, has_side_effects=True, vmem_limit_bytes=32 * 1024 * 1024
+        ),
+    )(
+        queries[0],
+        out_grad[0],
+        keys_values[0],
+        attn_output[0],
+        logsumexp[0],
+        segments,
+        layer_input[0],
+    )
+    return dq[None], dkv[None], weight
 
 
 def passed_along(shard, axis, by):
@@ -156,8 +461,9 @@
         P("dp", None),
         P("dp", ("blk", "uly"), None),
     )
+    small = tuple(mesh.shape[axis] for axis in ("uly", "blk", "dp")) == (2, 8, 2)
     return jax.shard_map(
-        on_device,
+        fused if small else on_device,
         mesh=mesh,
         in_specs=placed,
         out_specs=(

time: 212 us -> 50.3 us (0.24)
  waiting for transfers between devices: 146 us -> 0 us
  Pallas kernels: 0 us -> 41 us
  blocking collectives: 14.1 us -> 0 us
  between operations: 14.4 us -> 0.66 us
  starting transfers between devices: 12.2 us -> 0 us
  other arithmetic: 9.67 us -> 0 us
  matrix products: 4.83 us -> 0 us
    reduce_scatter x2 -> x0, waiting for transfers between devices: 136 us -> none  [the longest x1 124 us: on_device(): lax.psum_scatter(lax.dot_general(flat_input, value_grads, (((0,), (0,)),...]
    pallas_call x0 -> x1, Pallas kernels: none -> 41 us  [fused(): pl.pallas_call(fused_kernel, out_shape=(jax.ShapeDtypeStruct((CHUNK, widt...]
    all_to_all x1 -> x0, blocking collectives: 7.84 us -> none  [on_device(): lax.all_to_all(query_total.astype(jnp.bfloat16)[None], 'uly', split_axis=...]
    all_to_all x2 -> x0, starting transfers between devices: 6.89 us -> none  [the longest x1 3.44 us: on_device(): lax.all_to_all(queries, 'uly', split_axis=2, concat_axis=1, tiled=True)]
    unnamed x4 -> x0, other arithmetic: 6.72 us -> none
    all_gather x1 -> x0, blocking collectives: 6.24 us -> none  [on_device(): key_block = lax.all_gather(keys_values, 'uly', axis=1, tiled=True)[0]]
    ppermute x2 -> x0, waiting for transfers between devices: 5.67 us -> none  [passed_along(): return lax.ppermute(shard, axis, pairs)]
    ppermute x2 -> x0, starting transfers between devices: 5.2 us -> none  [passed_along(): return lax.ppermute(shard, axis, pairs)]
  transfers between devices with their start and end apart: 6 -> 0, of which waited for: 5 -> 0; matrix products, arithmetic and copies ran while one was open for 8% -> 0% of each run, Pallas kernels for 0% -> 0%
where the time goes in v1:
time: 50.3 us; the launch traced here: 49.9 us
  Pallas kernels  41 us (82%)
  local copies, waits for them, and re-layouts  8.25 us (16%)
  between operations  0.66 us (1%)
    pallas_call x1, Pallas kernels, fused(): pl.pallas_call(fused_kernel, out_shape=(jax.ShapeDtypeStruct((CHUNK, widt...  41 us
    unnamed x17, local copies, waits for them, and re-layouts  8.25 us

profile of v1, /device:TPU:0, one launch (start us, length us, event | category | flops | bytes accessed | tf_op | source)
XLA Modules:
  0.0 49.9 jit_solution(11740565915390765124)
XLA Ops:
  0.6 0.0 copy-start.5
  0.6 0.7 %copy-done.5 = s32[1,2048]{1,0:T(1,128)S(1)} copy-done((s32[1,2048]{1,0:T(1,128)S(1)}, s32[1,2048]{1,0:T(1,128)}, u32[]{:S(2)}) %copy-start.5) | copy-done | bytes 8216
  1.3 0.0 copy-start
  1.3 1.2 %copy-done = bf16[1,128,4096]{2,1,0:T(8,128)(2,1)S(1)} copy-done((bf16[1,128,4096]{2,1,0:T(8,128)(2,1)S(1)}, bf16[1,128,4096]{2,1,0:T(8,128)(2,1)}, u32[]{:S(2)}) %copy-start) | copy-done | bytes 1048600
  2.6 0.0 copy-start.1
  2.6 0.9 %copy-done.1 = bf16[1,128,1024]{2,1,0:T(8,128)(2,1)S(1)} copy-done((bf16[1,128,1024]{2,1,0:T(8,128)(2,1)S(1)}, bf16[1,128,1024]{2,1,0:T(8,128)(2,1)}, u32[]{:S(2)}) %copy-start.1) | copy-done | bytes 262168
  3.5 0.0 copy-start.2
  3.5 0.9 %copy-done.2 = bf16[1,128,1024]{2,1,0:T(8,128)(2,1)S(1)} copy-done((bf16[1,128,1024]{2,1,0:T(8,128)(2,1)S(1)}, bf16[1,128,1024]{2,1,0:T(8,128)(2,1)}, u32[]{:S(2)}) %copy-start.2) | copy-done | bytes 262168
  4.5 0.0 copy-start.3
  4.5 0.9 %copy-done.3 = bf16[1,4,256,128]{3,2,1,0:T(8,128)(2,1)S(1)} copy-done((bf16[1,4,256,128]{3,2,1,0:T(8,128)(2,1)S(1)}, bf16[1,4,256,128]{3,2,1,0:T(8,128)(2,1)}, u32[]{:S(2)}) %copy-start.3) | copy-done | bytes 262168
  5.4 0.0 copy-start.4
  5.4 0.8 %copy-done.4 = bf16[1,128,256]{2,1,0:T(8,128)(2,1)S(1)} copy-done((bf16[1,128,256]{2,1,0:T(8,128)(2,1)S(1)}, bf16[1,128,256]{2,1,0:T(8,128)(2,1)}, u32[]{:S(2)}) %copy-start.4) | copy-done | bytes 65560
  6.2 0.0 copy-start.6
  6.2 0.7 %copy-done.6 = f32[1,4,256]{2,1,0:T(4,128)S(1)} copy-done((f32[1,4,256]{2,1,0:T(4,128)S(1)}, f32[1,4,256]{2,1,0:T(4,128)}, u32[]{:S(2)}) %copy-start.6) | copy-done | bytes 4120
  6.9 41.0 %shard_map.94 = (bf16[128,1024]{1,0:T(8,128)(2,1)S(1)}, bf16[128,256]{1,0:T(8,128)(2,1)S(1)}, f32[128,128]{1,0:T(8,128)S(1)}) custom-call(bf16[128,1024]{1,0:T(8,128)(2,1)S(1)} %bitcast.10, bf16[128,1024]{1,0:T(8,128)(2,1)S(1)} %bitcast.11, bf16[128,256]{1,0:T(8,128)(2,1)S(1)} %bitcast.14, bf16[4,256,128]{2,1,0:T(8,128)(2,1)S(1)} %bitcast.12, ...), custom_call_target="tpu_custom_call" | custom-call | tf_op jit(solution)/shard_map/pallas_call | solution.py:257
  48.0 0.7 %copy.13 = bf16[1,128,1024]{2,1,0:T(8,128)(2,1)} copy(bf16[1,128,1024]{2,1,0:T(8,128)(2,1)S(1)} %bitcast.9) | data formatting | bytes 524288
  48.7 0.6 %copy.14 = bf16[1,128,256]{2,1,0:T(8,128)(2,1)} copy(bf16[1,128,256]{2,1,0:T(8,128)(2,1)S(1)} %bitcast.13) | data formatting | bytes 131072
  49.3 0.6 %copy.15 = f32[128,128]{1,0:T(8,128)} copy(f32[128,128]{1,0:T(8,128)S(1)} %get-tuple-element.14) | data formatting | bytes 131072
Async XLA Ops:
  0.6 0.7 %copy-start.5 = (s32[1,2048]{1,0:T(1,128)S(1)}, s32[1,2048]{1,0:T(1,128)}, u32[]{:S(2)}) copy-start(s32[1,2048]{1,0:T(1,128)} %seg_ref.1) | copy-start | bytes 24580
  1.3 1.2 %copy-start = (bf16[1,128,4096]{2,1,0:T(8,128)(2,1)S(1)}, bf16[1,128,4096]{2,1,0:T(8,128)(2,1)}, u32[]{:S(2)}) copy-start(bf16[1,128,4096]{2,1,0:T(8,128)(2,1)} %param.13) | copy-start | bytes 3145732
  2.6 0.9 %copy-start.1 = (bf16[1,128,1024]{2,1,0:T(8,128)(2,1)S(1)}, bf16[1,128,1024]{2,1,0:T(8,128)(2,1)}, u32[]{:S(2)}) copy-start(bf16[1,128,1024]{2,1,0:T(8,128)(2,1)} %param.7) | copy-start | bytes 786436
  3.5 0.9 %copy-start.2 = (bf16[1,128,1024]{2,1,0:T(8,128)(2,1)S(1)}, bf16[1,128,1024]{2,1,0:T(8,128)(2,1)}, u32[]{:S(2)}) copy-start(bf16[1,128,1024]{2,1,0:T(8,128)(2,1)} %param.8) | copy-start | bytes 786436
  4.5 0.9 %copy-start.3 = (bf16[1,4,256,128]{3,2,1,0:T(8,128)(2,1)S(1)}, bf16[1,4,256,128]{3,2,1,0:T(8,128)(2,1)}, u32[]{:S(2)}) copy-start(bf16[1,4,256,128]{3,2,1,0:T(8,128)(2,1)} %param.10) | copy-start | bytes 786436
  5.4 0.8 %copy-start.4 = (bf16[1,128,256]{2,1,0:T(8,128)(2,1)S(1)}, bf16[1,128,256]{2,1,0:T(8,128)(2,1)}, u32[]{:S(2)}) copy-start(bf16[1,128,256]{2,1,0:T(8,128)(2,1)} %param.9) | copy-start | bytes 196612
  6.2 0.7 %copy-start.6 = (f32[1,4,256]{2,1,0:T(4,128)S(1)}, f32[1,4,256]{2,1,0:T(4,128)}, u32[]{:S(2)}) copy-start(f32[1,4,256]{2,1,0:T(4,128)} %param.11) | copy-start | bytes 12292

commit v2 on v1

--- a/solution.py
+++ b/solution.py
@@ -11,8 +11,10 @@
 CHUNK = 128
 CHUNKS = 16
 SLOTS = 3
-GROUP = 16
+GROUP = 8
+CORNERS = 4
 HIDDEN = -1e30
+LOG2E = 1.4426950408889634
 
 
 def fused_kernel(
@@ -28,9 +30,11 @@
     w_ref,
     qs,
     gs,
-    kvb,
+    kb,
+    vb,
     ob,
     lb,
+    p_full,
     p_all,
     ds_all,
     send_kv,
@@ -38,6 +42,7 @@
     xin,
     vg,
     part,
+    part_low,
     part_in,
     q_sem,
     g_sem,
@@ -57,12 +62,14 @@
     p_recv,
 ):
     rows, head_dim = CHUNK, HEAD
+    low, full = jnp.bfloat16, jnp.float32
     uly = lax.axis_index("uly")
     blk = lax.axis_index("blk")
     dp = lax.axis_index("dp")
     chunk = blk * 2 + uly
     half = blk // 4
-    member = uly * 8 + (blk % 4) * 2 + dp
+    member = (blk % 4) * 2 + dp
+    corner = uly * 2 + half
 
     def at_chunk(index):
         index = lax.rem(index + CHUNKS, CHUNKS)
@@ -70,14 +77,21 @@
 
     def at_member(index):
         index = lax.rem(index, GROUP)
-        return {"uly": index // 8, "blk": half * 4 + (index % 8) // 2, "dp": index % 2}
+        return {"uly": uly, "blk": half * 4 + index // 2, "dp": index % 2}
+
+    def at_corner(index):
+        index = lax.rem(index, CORNERS)
+        return {"uly": index // 2, "blk": (index % 2) * 4 + blk % 4, "dp": dp}
 
     across = {"uly": 1 - uly, "blk": blk, "dp": dp}
-    mirror = {"uly": uly, "blk": lax.rem(blk + 4, 8), "dp": dp}
 
     def cols_of(index, side):
         index = lax.rem(index, GROUP)
-        return pl.ds(pl.multiple_of(((index // 8) * 16 + side * 8 + index % 8) * 128, 128), 128)
+        first = (side // 2) * 16 + (side % 2) * 8
+        return pl.ds(pl.multiple_of((first + index) * 128, 128), 128)
+
+    def lanes(side):
+        return pl.ds(side * 128, 128)
 
     loads = []
     for h in range(HEADS):
@@ -86,60 +100,27 @@
         loads.append(pltpu.make_async_copy(g_hbm.at[:, at_cols], gs.at[at_rows], g_sem.at[h]))
     mine = pl.ds(pl.multiple_of(uly * rows, rows), rows)
     theirs = pl.ds(pl.multiple_of((1 - uly) * rows, rows), rows)
-    loads.append(pltpu.make_async_copy(kv_hbm, kvb.at[pl.ds(0, rows)], own_sem.at[0]))
-    loads.append(pltpu.make_async_copy(o_hbm.at[:, mine], ob.at[uly], own_sem.at[1]))
-    loads.append(pltpu.make_async_copy(lse_hbm.at[:, mine], lb.at[uly], own_sem.at[2]))
-    for copy in loads:
-        copy.start()
+    own = pl.ds(0, rows)
+    keys_at, values_at = pl.ds(0, head_dim), pl.ds(head_dim, head_dim)
+    loads.append(pltpu.make_async_copy(kv_hbm.at[:, keys_at], kb.at[own], own_sem.at[0]))
+    loads.append(pltpu.make_async_copy(kv_hbm.at[:, values_at], vb.at[own], own_sem.at[1]))
+    loads.append(pltpu.make_async_copy(o_hbm.at[:, mine], ob.at[uly], own_sem.at[2]))
+    loads.append(pltpu.make_async_copy(lse_hbm.at[:, mine], lb.at[uly], own_sem.at[3]))
     x_own = [
-        pltpu.make_async_copy(x_hbm.at[:, cols_of(member, side)], xin.at[side, 0], x_own_sem.at[side])
-        for side in range(2)
+        pltpu.make_async_copy(
+            x_hbm.at[:, cols_of(member, side)], xin.at[0, :, lanes(side)], x_own_sem.at[side]
+        )
+        for side in range(CORNERS)
     ]
-    for copy in x_own:
-        copy.start()
 
     barrier = pltpu.get_barrier_semaphore()
     for step in (1, 2, -1, -2):
         pl.semaphore_signal(barrier, inc=1, device_id=at_chunk(chunk + step), device_id_type=MESH)
-    pl.semaphore_signal(barrier, inc=1, device_id=mirror, device_id_type=MESH)
+    for k in range(1, CORNERS):
+        pl.semaphore_signal(barrier, inc=1, device_id=at_corner(corner + k), device_id_type=MESH)
     for k in range(1, GROUP):
         pl.semaphore_signal(barrier, inc=1, device_id=at_member(member + k), device_id_type=MESH)
-    pl.semaphore_wait(barrier, GROUP - 1 + 5)
-
-    def remote(src, dst, send, recv, device):
-        return pltpu.make_async_remote_copy(
-            src_ref=src,
-            dst_ref=dst,
-            send_sem=send,
-            recv_sem=recv,
-            device_id=device,
-            device_id_type=MESH,
-        )
-
-    kv_out = [
-        remote(
-            kv_hbm, kvb.at[pl.ds(s * rows, rows)], kv_send.at[s - 1], kv_recv.at[s - 1], at_chunk(chunk + s)
-        )
-        for s in (1, 2)
-    ]
-    o_out = [
-        remote(o_hbm.at[:, theirs], ob.at[uly], o_send.at[0], o_recv.at[0], across),
-        remote(lse_hbm.at[:, theirs], lb.at[uly], o_send.at[1], o_recv.at[1], across),
-    ]
-    for copy in kv_out + o_out:
-        copy.start()
-    x_out = [
-        remote(
-            x_hbm.at[:, cols_of(member + k, side)],
-            xin.at[side, k],
-            x_send.at[side, k],
-            x_recv.at[side, k],
-            at_member(member + k),
-        )
-        for k in range(1, GROUP)
-        for side in range(2)
-    ]
-    for copy in x_out:
+    for copy in loads + x_own:
         copy.start()
 
     lane_query = lax.broadcasted_iota(jnp.int32, (rows, rows), 1)
@@ -160,92 +141,192 @@
     bias = jnp.concatenate(biases, axis=0)
     bias = jnp.concatenate([bias, bias], axis=1)
 
+    pl.semaphore_wait(barrier, GROUP - 1 + CORNERS - 1 + 4)
+
+    def remote(src, dst, send, recv, device):
+        return pltpu.make_async_remote_copy(
+            src_ref=src,
+            dst_ref=dst,
+            send_sem=send,
+            recv_sem=recv,
+            device_id=device,
+            device_id_type=MESH,
+        )
+
+    def to_chunks(columns, buffer, first):
+        return [
+            remote(
+                kv_hbm.at[:, columns],
+                buffer.at[pl.ds(s * rows, rows)],
+                kv_send.at[first + s - 1],
+                kv_recv.at[first + s - 1],
+                at_chunk(chunk + s),
+            )
+            for s in (1, 2)
+        ]
+
+    keys_out = to_chunks(keys_at, kb, 0)
+    lse_out = remote(lse_hbm.at[:, theirs], lb.at[uly], o_send.at[1], o_recv.at[1], across)
+    values_out = to_chunks(values_at, vb, 2)
+    o_out = remote(o_hbm.at[:, theirs], ob.at[uly], o_send.at[0], o_recv.at[0], across)
+    early, later = keys_out + [lse_out], values_out + [o_out]
+    for copy in early + later:
+        copy.start()
+    x_out = [
+        remote(
+            x_hbm.at[:, cols_of(member + k, side)],
+            xin.at[k, :, lanes(side)],
+            x_send.at[side, k],
+            x_recv.at[side, k],
+            at_member(member + k),
+        )
+        for k in range(1, GROUP)
+        for side in range(CORNERS)
+    ]
+    for copy in x_out:
+        copy.start()
+
     for copy in loads:
         copy.wait()
-    for copy in o_out + kv_out:
+    for copy in early:
         copy.wait_recv()
     scale = head_dim ** (-0.5)
     across_dims = (((1,), (1,)), ((), ()))
-    keys = kvb[:, :head_dim]
-    values = kvb[:, head_dim:]
-    for pair in range(HEADS // 2):
-        at_rows = slice(pair * 2 * rows, (pair + 1) * 2 * rows)
-        q_pair = qs[at_rows, :]
-        g_pair = gs[at_rows, :]
-        deltas, lses = [], []
+    pairs = [slice(pair * 2 * rows, (pair + 1) * 2 * rows) for pair in range(HEADS // 2)]
+
+    def probs_of(part_rows):
+        for pair, at_rows in enumerate(pairs):
+            lse = jnp.concatenate(
+                [lb[h // 4, h % 4 : h % 4 + 1, :] for h in (2 * pair, 2 * pair + 1)], axis=1
+            )
+            scores = lax.dot_general(
+                kb[part_rows, :], qs[at_rows, :], across_dims, preferred_element_type=full
+            )
+            prob = jnp.exp2(scores * (scale * LOG2E) - lse * LOG2E + bias[part_rows])
+            p_full[part_rows, at_rows] = prob
+            p_all[part_rows, at_rows] = prob.astype(low)
+
+    def returned(index):
+        return [
+            remote(
+                send_kv.at[index, s - 1],
+                recv_kv.at[index, s - 1],
+                ret_send.at[index, s - 1],
+                ret_recv.at[index, s - 1],
+                at_chunk(chunk - s),
+            )
+            for s in (1, 2)
+        ]
+
+    before, here = slice(rows, SLOTS * rows), slice(0, rows)
+    probs_of(before)
+    dv = jnp.dot(p_all[before, :], gs[...], preferred_element_type=full)
+    send_kv[0] = dv.astype(low).reshape(2, rows, head_dim)
+    dv_back = returned(0)
+    for copy in dv_back:
+        copy.start()
+    probs_of(here)
+    dv_own = jnp.dot(p_all[here, :], gs[...], preferred_element_type=full)
+
+    for copy in dv_back:
+        copy.wait_recv()
+    value_grad = dv_own + recv_kv[0, 0].astype(full) + recv_kv[0, 1].astype(full)
+    vg[0] = value_grad.T.astype(low)
+    v_out = [
+        remote(vg.at[0], vg.at[k], v_send.at[k], v_recv.at[k], at_member(member + k))
+        for k in range(1, GROUP)
+    ]
+    for copy in v_out:
+        copy.start()
+    dkv_ref[:, head_dim:] = value_grad.astype(low)
+
+    for copy in later:
+        copy.wait_recv()
+    for pair, at_rows in enumerate(pairs):
+        deltas = []
         for h in (2 * pair, 2 * pair + 1):
             prods = lax.dot_general(
                 ob[h // 4, h % 4],
                 gs[h * rows : (h + 1) * rows, :],
                 across_dims,
-                preferred_element_type=jnp.float32,
+                preferred_element_type=full,
             )
             deltas.append(
                 jnp.sum(jnp.where(row_key == lane_query, prods, 0.0), axis=0, keepdims=True)
             )
-            lses.append(lb[h // 4, h % 4 : h % 4 + 1, :])
         delta = jnp.concatenate(deltas, axis=1)
-        lse = jnp.concatenate(lses, axis=1)
-        scores = lax.dot_general(keys, q_pair, across_dims, preferred_element_type=jnp.float32)
-        dprob = lax.dot_general(values, g_pair, across_dims, preferred_element_type=jnp.float32)
-        prob = jnp.exp(scores * scale - lse + bias)
-        p_all[:, at_rows] = prob.astype(jnp.bfloat16)
-        ds_all[:, at_rows] = (prob * (dprob - delta)).astype(jnp.bfloat16)
-
-    dk = jnp.dot(ds_all[rows:, :], qs[...], preferred_element_type=jnp.float32) * scale
-    send_kv[:, :, :head_dim] = dk.reshape(2, rows, head_dim)
-    dv = jnp.dot(p_all[rows:, :], gs[...], preferred_element_type=jnp.float32)
-    send_kv[:, :, head_dim:] = dv.reshape(2, rows, head_dim)
-    returns = [
-        remote(send_kv.at[s - 1], recv_kv.at[s - 1], ret_send.at[s - 1], ret_recv.at[s - 1], at_chunk(chunk - s))
-        for s in (1, 2)
+        dprob = lax.dot_general(vb[...], gs[at_rows, :], across_dims, preferred_element_type=full)
+        ds_all[:, at_rows] = (p_full[:, at_rows] * (dprob - delta)).astype(low)
+    dk = jnp.dot(ds_all[before, :], qs[...], preferred_element_type=full) * scale
+    send_kv[1] = dk.astype(low).reshape(2, rows, head_dim)
+    dk_back = returned(1)
+    for copy in dk_back:
+        copy.start()
+
+    for copy in x_own:
+        copy.wait()
+    total = None
+    for first in range(0, GROUP, 2):
+        for k in (first, first + 1):
+            if k > 0:
+                v_out[k - 1].wait_recv()
+                for side in range(CORNERS):
+                    x_out[(k - 1) * CORNERS + side].wait_recv()
+        term = jnp.dot(
+            jnp.concatenate([vg[first], vg[first + 1]], axis=1),
+            xin[first : first + 2].reshape(2 * rows, CORNERS * 128),
+            preferred_element_type=full,
+        )
+        total = term if total is None else total + term
+    for side in range(CORNERS):
+        piece = total[:, side * 128 : (side + 1) * 128]
+        part[side] = piece
+        part_low[side] = piece.astype(low)
+    sums = [
+        remote(
+            part_low.at[lax.rem(corner + k, CORNERS)],
+            part_in.at[k],
+            p_send.at[k],
+            p_recv.at[k],
+            at_corner(corner + k),
+        )
+        for k in range(1, CORNERS)
     ]
-    for copy in returns:
-        copy.start()
-    dv_own = jnp.dot(p_all[:rows, :], gs[...], preferred_element_type=jnp.float32)
-    dk_own = jnp.dot(ds_all[:rows, :], qs[...], preferred_element_type=jnp.float32) * scale
+    for copy in sums:
+        copy.start()
+
+    dk_own = jnp.dot(ds_all[here, :], qs[...], preferred_element_type=full) * scale
     for h in range(HEADS):
         at_rows = slice(h * rows, (h + 1) * rows)
         dq = lax.dot_general(
-            ds_all[:, at_rows], keys, (((0,), (0,)), ((), ())), preferred_element_type=jnp.float32
-        )
-        dq_ref[:, at_rows] = (dq * scale).astype(jnp.bfloat16)
-
-    for copy in returns:
+            ds_all[:, at_rows], kb[...], (((0,), (0,)), ((), ())), preferred_element_type=full
+        )
+        dq_ref[:, at_rows] = (dq * scale).astype(low)
+    for copy in dk_back:
         copy.wait_recv()
-    value_grad = (dv_own + recv_kv[0, :, head_dim:] + recv_kv[1, :, head_dim:]).astype(jnp.bfloat16)
-    vg[0] = value_grad
-    v_out = [
-        remote(vg.at[0], vg.at[k], v_send.at[k], v_recv.at[k], at_member(member + k))
-        for k in range(1, GROUP)
+    dkv_ref[:, :head_dim] = (
+        dk_own + recv_kv[1, 0].astype(full) + recv_kv[1, 1].astype(full)
+    ).astype(low)
+    weight = part[corner]
+    for k, copy in enumerate(sums, 1):
+        copy.wait_recv()
+        weight = weight + part_in[k].astype(full)
+    w_ref[...] = weight.T * (rows * CHUNKS * 2) ** (-0.5)
+    for copy in early + later + x_out + dv_back + dk_back + v_out + sums:
+        copy.wait_send()
+
+
+def written(*refs):
+    half = len(refs) // 2
+    sources, results, sems = refs[:half], refs[half : 2 * half], refs[-1]
+    copies = [
+        pltpu.make_async_copy(source, result, sems.at[i])
+        for i, (source, result) in enumerate(zip(sources, results))
     ]
-    for copy in v_out:
-        copy.start()
-    dkv_ref[:, head_dim:] = value_grad
-    dkv_ref[:, :head_dim] = (dk_own + recv_kv[0, :, :head_dim] + recv_kv[1, :, :head_dim]).astype(
-        jnp.bfloat16
-    )
-
-    for copy in x_own:
+    for copy in copies:
+        copy.start()
+    for copy in copies:
         copy.wait()
-    for copy in x_out:
-        copy.wait_recv()
-    for copy in v_out:
-        copy.wait_recv()
-    grads = vg[...].reshape(GROUP * rows, head_dim)
-    for side in range(2):
-        part[side] = lax.dot_general(
-            xin[side].reshape(GROUP * rows, 128),
-            grads,
-            (((0,), (0,)), ((), ())),
-            preferred_element_type=jnp.float32,
-        )
-    swap = remote(part.at[1 - half], part_in, p_send.at[0], p_recv.at[0], mirror)
-    swap.start()
-    swap.wait_recv()
-    w_ref[...] = (part[half] + part_in[...]) * (rows * CHUNKS * 2) ** (-0.5)
-    for copy in kv_out + o_out + x_out + returns + v_out + [swap]:
-        copy.wait_send()
 
 
 def fused(queries, out_grad, keys_values, attn_output, logsumexp, segments, layer_input):
@@ -254,48 +335,52 @@
     low, full = jnp.bfloat16, jnp.float32
     dma = pltpu.SemaphoreType.DMA
     width = HEADS * HEAD
-    dq, dkv, weight = pl.pallas_call(
+    results = (
+        jax.ShapeDtypeStruct((CHUNK, width), low),
+        jax.ShapeDtypeStruct((CHUNK, 2 * HEAD), low),
+        jax.ShapeDtypeStruct((128, HEAD), full),
+    )
+    found = pl.pallas_call(
         fused_kernel,
-        out_shape=(
-            jax.ShapeDtypeStruct((CHUNK, width), low),
-            jax.ShapeDtypeStruct((CHUNK, 2 * HEAD), low),
-            jax.ShapeDtypeStruct((128, HEAD), full),
-        ),
+        out_shape=results,
         in_specs=[anywhere] * 5 + [in_vmem, anywhere],
         out_specs=(in_vmem, in_vmem, in_vmem),
         scratch_shapes=[
             pltpu.VMEM((width, HEAD), low),
             pltpu.VMEM((width, HEAD), low),
-            pltpu.VMEM((SLOTS * CHUNK, 2 * HEAD), low),
+            pltpu.VMEM((SLOTS * CHUNK, HEAD), low),
+            pltpu.VMEM((SLOTS * CHUNK, HEAD), low),
             pltpu.VMEM((2, HEADS // 2, CHUNK, HEAD), low),
             pltpu.VMEM((2, HEADS // 2, CHUNK), full),
+            pltpu.VMEM((SLOTS * CHUNK, width), full),
             pltpu.VMEM((SLOTS * CHUNK, width), low),
             pltpu.VMEM((SLOTS * CHUNK, width), low),
-            pltpu.VMEM((2, CHUNK, 2 * HEAD), full),
-            pltpu.VMEM((2, CHUNK, 2 * HEAD), full),
-            pltpu.VMEM((2, GROUP, CHUNK, 128), low),
-            pltpu.VMEM((GROUP, CHUNK, HEAD), low),
-            pltpu.VMEM((2, 128, HEAD), full),
-            pltpu.VMEM((128, HEAD), full),
+            pltpu.VMEM((2, 2, CHUNK, HEAD), low),
+            pltpu.VMEM((2, 2, CHUNK, HEAD), low),
+            pltpu.VMEM((GROUP, CHUNK, CORNERS * 128), low),
+            pltpu.VMEM((GROUP, HEAD, CHUNK), low),
+            pltpu.VMEM((CORNERS, HEAD, 128), full),
+            pltpu.VMEM((CORNERS, HEAD, 128), low),
+            pltpu.VMEM((CORNERS, HEAD, 128), low),
             dma((HEADS,)),
             dma((HEADS,)),
-            dma((3,)),
+            dma((4,)),
+            dma((CORNERS,)),
+            dma((4,)),
+            dma((4,)),
             dma((2,)),
             dma((2,)),
-            dma((2,)),
-            dma((2,)),
-            dma((2,)),
-            dma((2,)),
-            dma((2,)),
-            dma((2, GROUP)),
-            dma((2, GROUP)),
+            dma((2, 2)),
+            dma((2, 2)),
+            dma((CORNERS, GROUP)),
+            dma((CORNERS, GROUP)),
             dma((GROUP,)),
             dma((GROUP,)),
-            dma((1,)),
-            dma((1,)),
+            dma((CORNERS,)),
+            dma((CORNERS,)),
         ],
         compiler_params=pltpu.CompilerParams(
-            collective_id=0, has_side_effects=True, vmem_limit_bytes=32 * 1024 * 1024
+            collective_id=0, has_side_effects=True, vmem_limit_bytes=60 * 1024 * 1024
         ),
     )(
         queries[0],
@@ -306,6 +391,13 @@
         segments,
         layer_input[0],
     )
+    dq, dkv, weight = pl.pallas_call(
+        written,
+        out_shape=results,
+        in_specs=[anywhere] * 3,
+        out_specs=(anywhere,) * 3,
+        scratch_shapes=[dma((3,))],
+    )(*found)
     return dq[None], dkv[None], weight
 
 

time: 50.3 us -> 48.9 us (0.972)
  local copies, waits for them, and re-layouts: 8.25 us -> 0 us
  Pallas kernels: 41 us -> 48 us
    unnamed x17 -> x0, local copies, waits for them, and re-layouts: 8.25 us -> none
    pallas_call x1 -> x2, Pallas kernels: 41 us -> 48 us  [the longest x1 35 us: fused(): pl.pallas_call(fused_kernel, out_shape=results, in_specs=[anywhere] * 5 +...]
where the time goes in v2:
time: 48.9 us; the launch traced here: 48.7 us
  Pallas kernels  48 us (98%)
  between operations  0.64 us (1%)
    pallas_call x1, Pallas kernels, fused(): pl.pallas_call(fused_kernel, out_shape=results, in_specs=[anywhere] * 5 +...  35 us
    pallas_call x1, Pallas kernels, fused(): pl.pallas_call(written, out_shape=results, in_specs=[anywhere] * 3, out_s...  13 us

profile of v2, /device:TPU:0, one launch (start us, length us, event | category | flops | bytes accessed | tf_op | source)
XLA Modules:
  0.0 48.7 jit_solution(11286296529586587124)
XLA Ops:
  0.6 35.0 %shard_map.94 = (bf16[128,1024]{1,0:T(8,128)(2,1)}, bf16[128,256]{1,0:T(8,128)(2,1)}, f32[128,128]{1,0:T(8,128)}) custom-call(bf16[128,1024]{1,0:T(8,128)(2,1)} %bitcast.9, bf16[128,1024]{1,0:T(8,128)(2,1)} %bitcast.10, bf16[128,256]{1,0:T(8,128)(2,1)} %bitcast.12, bf16[4,256,128]{2,1,0:T(8,128)(2,1)} %bitcast.11, f32[4,256]{1,0:T(4,128)} %bitcast.13, ...), custom_call_target="tpu_custom_call" | custom-call | tf_op jit(solution)/shard_map/pallas_call | solution.py:343
  35.6 13.0 %shard_map.95 = (bf16[128,1024]{1,0:T(8,128)(2,1)}, bf16[128,256]{1,0:T(8,128)(2,1)}, f32[128,128]{1,0:T(8,128)}) custom-call(bf16[128,1024]{1,0:T(8,128)(2,1)} %get-tuple-element.9.refs_0_, bf16[128,256]{1,0:T(8,128)(2,1)} %get-tuple-element.10.refs_1_, f32[128,128]{1,0:T(8,128)} %get-tuple-element.11.refs_2_), custom_call_target="tpu_custom_call" | custom-call | tf_op jit(solution)/shard_map/pallas_call | solution.py:394

commit v3 on v2

--- a/solution.py
+++ b/solution.py
@@ -13,6 +13,7 @@
 SLOTS = 3
 GROUP = 8
 CORNERS = 4
+FIRST, SECOND, THIRD = (1, 2, 3), (4, 5), (6, 7)
 HIDDEN = -1e30
 LOG2E = 1.4426950408889634
 
@@ -183,8 +184,13 @@
         for k in range(1, GROUP)
         for side in range(CORNERS)
     ]
-    for copy in x_out:
-        copy.start()
+
+    def start_inputs(peers):
+        for k in peers:
+            for copy in x_out[(k - 1) * CORNERS : k * CORNERS]:
+                copy.start()
+
+    start_inputs(FIRST)
 
     for copy in loads:
         copy.wait()
@@ -225,6 +231,7 @@
     dv_back = returned(0)
     for copy in dv_back:
         copy.start()
+    start_inputs(SECOND)
     probs_of(here)
     dv_own = jnp.dot(p_all[here, :], gs[...], preferred_element_type=full)
 
@@ -238,6 +245,7 @@
     ]
     for copy in v_out:
         copy.start()
+    start_inputs(THIRD)
     dkv_ref[:, head_dim:] = value_grad.astype(low)
 
     for copy in later:
@@ -263,6 +271,19 @@
     for copy in dk_back:
         copy.start()
 
+    dk_own = jnp.dot(ds_all[here, :], qs[...], preferred_element_type=full) * scale
+    for h in range(HEADS):
+        at_rows = slice(h * rows, (h + 1) * rows)
+        dq = lax.dot_general(
+            ds_all[:, at_rows], kb[...], (((0,), (0,)), ((), ())), preferred_element_type=full
+        )
+        dq_ref[:, at_rows] = (dq * scale).astype(low)
+    for copy in dk_back:
+        copy.wait_recv()
+    dkv_ref[:, :head_dim] = (
+        dk_own + recv_kv[1, 0].astype(full) + recv_kv[1, 1].astype(full)
+    ).astype(low)
+
     for copy in x_own:
         copy.wait()
     total = None
@@ -295,18 +316,6 @@
     for copy in sums:
         copy.start()
 
-    dk_own = jnp.dot(ds_all[here, :], qs[...], preferred_element_type=full) * scale
-    for h in range(HEADS):
-        at_rows = slice(h * rows, (h + 1) * rows)
-        dq = lax.dot_general(
-            ds_all[:, at_rows], kb[...], (((0,), (0,)), ((), ())), preferred_element_type=full
-        )
-        dq_ref[:, at_rows] = (dq * scale).astype(low)
-    for copy in dk_back:
-        copy.wait_recv()
-    dkv_ref[:, :head_dim] = (
-        dk_own + recv_kv[1, 0].astype(full) + recv_kv[1, 1].astype(full)
-    ).astype(low)
     weight = part[corner]
     for k, copy in enumerate(sums, 1):
         copy.wait_recv()
@@ -316,17 +325,10 @@
         copy.wait_send()
 
 
-def written(*refs):
-    half = len(refs) // 2
-    sources, results, sems = refs[:half], refs[half : 2 * half], refs[-1]
-    copies = [
-        pltpu.make_async_copy(source, result, sems.at[i])
-        for i, (source, result) in enumerate(zip(sources, results))
-    ]
-    for copy in copies:
-        copy.start()
-    for copy in copies:
-        copy.wait()
+def written(dq_ref, dkv_ref, w_ref, dq_out, dkv_out, w_out):
+    dq_out[...] = dq_ref[...]
+    dkv_out[...] = dkv_ref[...]
+    w_out[...] = w_ref[...]
 
 
 def fused(queries, out_grad, keys_values, attn_output, logsumexp, segments, layer_input):
@@ -394,9 +396,8 @@
     dq, dkv, weight = pl.pallas_call(
         written,
         out_shape=results,
-        in_specs=[anywhere] * 3,
-        out_specs=(anywhere,) * 3,
-        scratch_shapes=[dma((3,))],
+        in_specs=[in_vmem] * 3,
+        out_specs=(in_vmem,) * 3,
     )(*found)
     return dq[None], dkv[None], weight
 

time: 48.9 us -> 37.2 us (0.76)
  Pallas kernels: 48 us -> 36.4 us
    pallas_call x1, Pallas kernels: 13 us -> 1.73 us  [fused(): pl.pallas_call(written, out_shape=results, in_specs=[in_vmem] * 3, out_sp...]
where the time goes in v3:
time: 37.2 us; the launch traced here: 37 us
  Pallas kernels  36.4 us (98%)
  between operations  0.64 us (2%)
    pallas_call x1, Pallas kernels, fused(): pl.pallas_call(fused_kernel, out_shape=results, in_specs=[anywhere] * 5 +...  34.6 us
    pallas_call x1, Pallas kernels, fused(): pl.pallas_call(written, out_shape=results, in_specs=[in_vmem] * 3, out_sp...  1.73 us

profile of v3, /device:TPU:0, one launch (start us, length us, event | category | flops | bytes accessed | tf_op | source)
XLA Modules:
  0.0 37.0 jit_solution(15087788479091931019)
XLA Ops:
  0.6 34.6 %shard_map.94 = (bf16[128,1024]{1,0:T(8,128)(2,1)}, bf16[128,256]{1,0:T(8,128)(2,1)}, f32[128,128]{1,0:T(8,128)}) custom-call(bf16[128,1024]{1,0:T(8,128)(2,1)} %bitcast.9, bf16[128,1024]{1,0:T(8,128)(2,1)} %bitcast.10, bf16[128,256]{1,0:T(8,128)(2,1)} %bitcast.12, bf16[4,256,128]{2,1,0:T(8,128)(2,1)} %bitcast.11, f32[4,256]{1,0:T(4,128)} %bitcast.13, ...), custom_call_target="tpu_custom_call" | custom-call | tf_op jit(solution)/shard_map/pallas_call | solution.py:345
  35.3 1.7 %shard_map.95 = (bf16[128,1024]{1,0:T(8,128)(2,1)}, bf16[128,256]{1,0:T(8,128)(2,1)}, f32[128,128]{1,0:T(8,128)}) custom-call(bf16[128,1024]{1,0:T(8,128)(2,1)} %get-tuple-element.9.dq_ref, bf16[128,256]{1,0:T(8,128)(2,1)} %get-tuple-element.10.dkv_ref, f32[128,128]{1,0:T(8,128)} %get-tuple-element.11.w_ref), custom_call_target="tpu_custom_call" | custom-call | tf_op jit(solution)/shard_map/pallas_call | solution.py:396

commit v4 on v3

--- a/solution.py
+++ b/solution.py
@@ -278,12 +278,6 @@
             ds_all[:, at_rows], kb[...], (((0,), (0,)), ((), ())), preferred_element_type=full
         )
         dq_ref[:, at_rows] = (dq * scale).astype(low)
-    for copy in dk_back:
-        copy.wait_recv()
-    dkv_ref[:, :head_dim] = (
-        dk_own + recv_kv[1, 0].astype(full) + recv_kv[1, 1].astype(full)
-    ).astype(low)
-
     for copy in x_own:
         copy.wait()
     total = None
@@ -315,6 +309,12 @@
     ]
     for copy in sums:
         copy.start()
+
+    for copy in dk_back:
+        copy.wait_recv()
+    dkv_ref[:, :head_dim] = (
+        dk_own + recv_kv[1, 0].astype(full) + recv_kv[1, 1].astype(full)
+    ).astype(low)
 
     weight = part[corner]
     for k, copy in enumerate(sums, 1):

time: 37.2 us -> 35.9 us (0.965)
  the two profiles are of different devices: /device:TPU:0 before, /device:TPU:1 now
where the time goes in v4:
time: 35.9 us; the launch traced here: 35.7 us
  Pallas kernels  35.1 us (98%)
  between operations  0.64 us (2%)
    pallas_call x1, Pallas kernels, fused(): pl.pallas_call(fused_kernel, out_shape=results, in_specs=[anywhere] * 5 +...  33.4 us
    pallas_call x1, Pallas kernels, fused(): pl.pallas_call(written, out_shape=results, in_specs=[in_vmem] * 3, out_sp...  1.73 us

profile of v4, /device:TPU:1, one launch (start us, length us, event | category | flops | bytes accessed | tf_op | source)
XLA Modules:
  0.0 35.7 jit_solution(10221730734449711359)
XLA Ops:
  0.6 33.4 %shard_map.94 = (bf16[128,1024]{1,0:T(8,128)(2,1)}, bf16[128,256]{1,0:T(8,128)(2,1)}, f32[128,128]{1,0:T(8,128)}) custom-call(bf16[128,1024]{1,0:T(8,128)(2,1)} %bitcast.9, bf16[128,1024]{1,0:T(8,128)(2,1)} %bitcast.10, bf16[128,256]{1,0:T(8,128)(2,1)} %bitcast.12, bf16[4,256,128]{2,1,0:T(8,128)(2,1)} %bitcast.11, f32[4,256]{1,0:T(4,128)} %bitcast.13, ...), custom_call_target="tpu_custom_call" | custom-call | tf_op jit(solution)/shard_map/pallas_call | solution.py:345
  34.0 1.7 %shard_map.95 = (bf16[128,1024]{1,0:T(8,128)(2,1)}, bf16[128,256]{1,0:T(8,128)(2,1)}, f32[128,128]{1,0:T(8,128)}) custom-call(bf16[128,1024]{1,0:T(8,128)(2,1)} %get-tuple-element.9.dq_ref, bf16[128,256]{1,0:T(8,128)(2,1)} %get-tuple-element.10.dkv_ref, f32[128,128]{1,0:T(8,128)} %get-tuple-element.11.w_ref), custom_call_target="tpu_custom_call" | custom-call | tf_op jit(solution)/shard_map/pallas_call | solution.py:396
